TPU v7x, 512 devices: a whole 4x8x8 slice. The times are simulated.
512 devices in a mesh: freq: 8 (over z), sx: 16 (over y, core), sy: 4 (over x).
Axes of the slice: x: 4, y: 8, z: 8, core: 2. Of those that a mesh axis runs over, the one named last changes fastest.
Arguments:
- stiffness: bfloat16 [16, 4, 3072, 3072], P('sx', 'sy', None, 'freq')
- mass_matrix: bfloat16 [16, 4, 3072, 3072], P('sx', 'sy', None, 'freq')
- omega_table: float32 [32], replicated, may hold values from 0.5 to 6
- assignment: int32 [32], P('freq'), may hold values from 0 to 31, each once
- adjoint_load: float32 [16, 4, 32, 2, 4, 768], P('sx', 'sy', 'freq'), as said below
- forward_state: bfloat16 [16, 4, 32, 2, 4, 768], P('sx', 'sy', 'freq'), may hold values from -6 to 6
- owner_index: int32 [16, 4, 4, 768], P('sx', 'sy'), may hold values from 0 to 1727
Outputs:
- adjoint: float32 [16, 4, 32, 2, 4, 768], P('sx', 'sy', 'freq')
- gradient: float32 [16, 4, 1728], P('sx', 'sy', 'freq')
- residual_level: float32 [32], P('freq')
Inputs may be any that keep to these rules, and one draw needn't show every extreme that they name: `adjoint_load`: the two copies of a face shared by neighbouring substructures are equal.
All inputs are finite; a program needn't handle non-finite values.
Results may differ from a plain program's by a relative error of at most 0.012.
Values may be sent and summed in bfloat16 or wider, within the bound.
No kernel may reach another device: no remote copies, remote signals or barrier semaphores. Data moves between devices by JAX's collectives and lax.ppermute only.
A program may use at most 64 MiB of HBM per device.

v0:
```python
import jax
import jax.numpy as jnp
from jax import lax
from jax.sharding import PartitionSpec as P

ITERS = 4
DE_SUB = 1728
LOSS_FACTOR = 0.3


def padded(cells, sides, width):
    for axis, dim in sides:
        count = lax.axis_size(axis)
        ends = count - 1
        head = lax.slice_in_dim(cells, 0, width, axis=dim)
        tail = lax.slice_in_dim(cells, cells.shape[dim] - width, cells.shape[dim], axis=dim)
        cells = jnp.concatenate(
            [
                lax.ppermute(tail, axis, [(i, (i + 1) % count) for i in range(ends)]),
                cells,
                lax.ppermute(head, axis, [((i + 1) % count, i) for i in range(ends)]),
            ],
            axis=dim,
        )
    return cells


def face_weights():
    index_x = lax.axis_index("sx")
    size_x = lax.axis_size("sx")
    index_y = lax.axis_index("sy")
    size_y = lax.axis_size("sy")
    west_weight = jnp.where(index_x > 0, 0.5, 1.0)
    east_weight = jnp.where(index_x < size_x - 1, 0.5, 1.0)
    south_weight = jnp.where(index_y > 0, 0.5, 1.0)
    north_weight = jnp.where(index_y < size_y - 1, 0.5, 1.0)
    return jnp.stack([west_weight, east_weight, south_weight, north_weight]).astype(jnp.float32)


def assemble(local_vals):
    padded_x = padded(local_vals[:, :, 0:2].astype(jnp.bfloat16), (("sx", 2),), 1).astype(
        jnp.float32
    )
    padded_y = padded(local_vals[:, :, 2:4].astype(jnp.bfloat16), (("sy", 2),), 1).astype(
        jnp.float32
    )
    west_face = padded_x[:, :, 1] + padded_x[:, :, 0]
    east_face = padded_x[:, :, 2] + padded_x[:, :, 3]
    south_face = padded_y[:, :, 1] + padded_y[:, :, 0]
    north_face = padded_y[:, :, 2] + padded_y[:, :, 3]
    return jnp.stack([west_face, east_face, south_face, north_face], axis=2)


def mix_parts(stiff_part, mass_part, omega_sq, sign_factor):
    factor = omega_sq[:, None, None]
    real_part = (
        stiff_part[:, 0] - sign_factor * LOSS_FACTOR * stiff_part[:, 1] - factor * mass_part[:, 0]
    )
    imag_part = (
        stiff_part[:, 1] + sign_factor * LOSS_FACTOR * stiff_part[:, 0] - factor * mass_part[:, 1]
    )
    return jnp.stack([real_part, imag_part], axis=1)


def apply_rows(vector, stiff_cols, mass_cols, omega_every, sign_factor):
    face_count = vector.shape[2]
    matrix_order = face_count * vector.shape[3]
    rounded = vector.astype(jnp.bfloat16)
    pieces = lax.all_gather(rounded, "freq", axis=0, tiled=True)
    count = pieces.shape[0]
    flattened = pieces.reshape(-1, matrix_order)
    stiff_part = jnp.dot(flattened, stiff_cols, preferred_element_type=jnp.float32)
    mass_part = jnp.dot(flattened, mass_cols, preferred_element_type=jnp.float32)
    local_vals = mix_parts(
        stiff_part.reshape(count, 2, face_count, -1),
        mass_part.reshape(count, 2, face_count, -1),
        omega_every,
        sign_factor,
    )
    returned = lax.all_to_all(
        local_vals.astype(jnp.bfloat16), "freq", split_axis=0, concat_axis=3, tiled=True
    ).astype(local_vals.dtype)
    return assemble(returned)


def reduce_dots(factor_pairs, weights):
    partial_value = tuple(
        (
            jnp.sum(first_vec * second_vec * weights[None, None, :, None], axis=(1, 2, 3))
            for first_vec, second_vec in factor_pairs
        )
    )
    summed = lax.psum(partial_value, ("sx", "sy"))
    return summed


def per_freq(values):
    return values[:, None, None, None]


def face_columns(matrix, matrix_order, face_count):
    grouped = matrix.reshape(matrix_order, -1, face_count)
    return jnp.swapaxes(grouped, 1, 2).reshape(matrix_order, -1)


def body(stiffness, mass_matrix, omega_table, assignment, adjoint_load, forward_state, owner_index):
    n_freq = lax.axis_size("freq")
    slot_count = adjoint_load.shape[2]
    face_count = adjoint_load.shape[4]
    face_len = adjoint_load.shape[5]
    matrix_order = face_count * face_len
    stiff_cols = face_columns(stiffness[0, 0], matrix_order, face_count)
    mass_cols = face_columns(mass_matrix[0, 0], matrix_order, face_count)
    matches = assignment[:, None] == jnp.arange(omega_table.shape[0], dtype=jnp.int32)[None, :]
    slot_omega = jnp.sum(jnp.where(matches, omega_table[None, :], 0.0), axis=1)
    weights = face_weights()
    load_rows = adjoint_load[0, 0]
    omega_every = lax.all_gather(slot_omega, "freq", axis=0, tiled=True)

    def operate(vector, sign_factor):
        return apply_rows(vector, stiff_cols, mass_cols, omega_every, sign_factor)

    residual = load_rows
    solution = jnp.zeros_like(load_rows)
    normal_res = operate(residual, -1.0)
    direction = normal_res
    gamma_now = reduce_dots(((normal_res, normal_res),), weights)[0]
    for iteration in range(ITERS):
        image_vec = operate(direction, 1.0)
        delta_now = reduce_dots(((image_vec, image_vec),), weights)[0]
        step_size = gamma_now / delta_now
        solution = solution + per_freq(step_size) * direction
        if iteration + 1 < ITERS:
            residual = residual - per_freq(step_size) * image_vec
            normal_res = operate(residual, -1.0)
            gamma_next = reduce_dots(((normal_res, normal_res),), weights)[0]
            direction = normal_res + per_freq(gamma_next / gamma_now) * direction
            gamma_now = gamma_next
    cell_count = float(lax.axis_size("sx") * lax.axis_size("sy") * 2 * matrix_order)
    residual_level = jnp.log(gamma_now / cell_count)
    state_vec = forward_state[0, 0].astype(jnp.float32)
    lambda_real = solution[:, 0]
    lambda_imag = solution[:, 1]
    state_real = state_vec[:, 0]
    state_imag = state_vec[:, 1]
    product_term = (
        lambda_real * state_real
        - lambda_imag * state_imag
        - LOSS_FACTOR * (lambda_real * state_imag + lambda_imag * state_real)
    )
    dof_total = jnp.sum(product_term, axis=0)
    partial_grad = jax.ops.segment_sum(
        dof_total.reshape(-1), owner_index[0, 0].reshape(-1), num_segments=DE_SUB
    )
    grad_factor = (DE_SUB / (slot_count * n_freq * matrix_order)) ** 0.5
    gradient = lax.psum_scatter(
        -grad_factor * partial_grad, "freq", scatter_dimension=0, tiled=True
    )
    return (solution[None, None], gradient[None, None], residual_level)


def solution(mesh):
    return jax.shard_map(
        body,
        mesh=mesh,
        in_specs=(
            P("sx", "sy", None, "freq"),
            P("sx", "sy", None, "freq"),
            P(),
            P("freq"),
            P("sx", "sy", "freq", None, None, None),
            P("sx", "sy", "freq", None, None, None),
            P("sx", "sy", None, None),
        ),
        out_specs=(P("sx", "sy", "freq", None, None, None), P("sx", "sy", "freq"), P("freq")),
        check_vma=False,
    )
```

profile of v0, /device:TPU:32, one launch (start us, length us, event | category | flops | bytes accessed | tf_op | source)
XLA Modules:
  0.0 1387.7 jit_solution(9510212069884050593)
XLA Ops:
  5.9 31.4 %all_gather.27 = bf16[32,2,4,768]{3,2,1,0:T(4,128)(2,1)S(1)} all-gather(bf16[4,2,4,768]{3,2,1,0:T(4,128)(2,1)S(1)} %bitcast_convert_fusion), channel_id=1, replica_groups=mesh['freq'=8,'sx'=16,'sy'=4] {'freq'}, dimensions={0}, use_global_device_ids=true | all-gather | bytes 442368 | tf_op jit(solution)/shard_map/all_gather | solution.py:69
  48.3 17.0 %all-reduce = f32[32]{0:T(128)S(1)} all-reduce(f32[32]{0:T(128)S(1)} %dynamic-update-slice), channel_id=1, replica_groups=mesh['freq'=8,'sx'=16,'sy'=4] {'freq'}, use_global_device_ids=true, to_apply=%add | all-reduce | flops 32 | bytes 256
  69.5 8.3 all-to-all-done
  83.7 4.5 collective-permute-start.2
  90.1 25.1 %all_gather.29 = bf16[32,2,4,768]{3,2,1,0:T(4,128)(2,1)S(1)} all-gather(bf16[4,2,4,768]{3,2,1,0:T(4,128)(2,1)S(1)} %fusion.103), channel_id=1, replica_groups=mesh['freq'=8,'sx'=16,'sy'=4] {'freq'}, dimensions={0}, use_global_device_ids=true | all-gather | bytes 442368 | tf_op jit(solution)/shard_map/all_gather | solution.py:69
  122.3 8.2 all-to-all-done.1
  132.1 5.0 collective-permute-start.6
  145.9 126.0 %all-reduce.2 = (f32[4]{0:T(128)S(1)}, f32[4]{0:T(128)S(1)}) all-reduce(f32[4]{0:T(128)S(1)} %get-tuple-element.4, f32[4]{0:T(128)S(1)} %get-tuple-element.3), channel_id=1, replica_groups=mesh['freq'=8,'sx'=16,'sy'=4] {'sx','sy'}, use_global_device_ids=true, to_apply=%region_2.3 | all-reduce | flops 8 | bytes 64 | tf_op jit(solution)/shard_map/psum | solution.py:93
  272.1 25.5 %all_gather.30 = bf16[32,2,4,768]{3,2,1,0:T(4,128)(2,1)S(1)} all-gather(bf16[4,2,4,768]{3,2,1,0:T(4,128)(2,1)S(1)} %get-tuple-element.13), channel_id=1, replica_groups=mesh['freq'=8,'sx'=16,'sy'=4] {'freq'}, dimensions={0}, use_global_device_ids=true | all-gather | bytes 442368 | tf_op jit(solution)/shard_map/all_gather | solution.py:69
  300.6 10.8 all_to_all.32
  312.9 4.5 collective-permute-start.10
  326.2 124.5 %psum.58 = f32[4]{0:T(128)S(1)} all-reduce(f32[4]{0:T(128)S(1)} %multiply_reduce_fusion.4), channel_id=1, replica_groups=mesh['freq'=8,'sx'=16,'sy'=4] {'sx','sy'}, use_global_device_ids=true, to_apply=%region_6.7 | all-reduce | flops 4 | bytes 32 | tf_op jit(solution)/shard_map/psum | solution.py:93
  450.9 25.0 %all_gather.31 = bf16[32,2,4,768]{3,2,1,0:T(4,128)(2,1)S(1)} all-gather(bf16[4,2,4,768]{3,2,1,0:T(4,128)(2,1)S(1)} %get-tuple-element.11), channel_id=1, replica_groups=mesh['freq'=8,'sx'=16,'sy'=4] {'freq'}, dimensions={0}, use_global_device_ids=true | all-gather | bytes 442368 | tf_op jit(solution)/shard_map/all_gather | solution.py:69
  479.0 11.0 all_to_all.33
  491.6 5.1 collective-permute-start.14
  505.4 126.1 %psum.59 = f32[4]{0:T(128)S(1)} all-reduce(f32[4]{0:T(128)S(1)} %multiply_reduce_fusion.3), channel_id=1, replica_groups=mesh['freq'=8,'sx'=16,'sy'=4] {'sx','sy'}, use_global_device_ids=true, to_apply=%region_8.9 | all-reduce | flops 4 | bytes 32 | tf_op jit(solution)/shard_map/psum | solution.py:93
  632.2 25.5 %all_gather.32 = bf16[32,2,4,768]{3,2,1,0:T(4,128)(2,1)S(1)} all-gather(bf16[4,2,4,768]{3,2,1,0:T(4,128)(2,1)S(1)} %get-tuple-element.9), channel_id=1, replica_groups=mesh['freq'=8,'sx'=16,'sy'=4] {'freq'}, dimensions={0}, use_global_device_ids=true | all-gather | bytes 442368 | tf_op jit(solution)/shard_map/all_gather | solution.py:69
  660.7 10.8 all_to_all.34
  686.3 124.3 %psum.60 = f32[4]{0:T(128)S(1)} all-reduce(f32[4]{0:T(128)S(1)} %multiply_reduce_fusion.2), channel_id=1, replica_groups=mesh['freq'=8,'sx'=16,'sy'=4] {'sx','sy'}, use_global_device_ids=true, to_apply=%region_10.11 | all-reduce | flops 4 | bytes 32 | tf_op jit(solution)/shard_map/psum | solution.py:93
  811.1 25.0 %all_gather.33 = bf16[32,2,4,768]{3,2,1,0:T(4,128)(2,1)S(1)} all-gather(bf16[4,2,4,768]{3,2,1,0:T(4,128)(2,1)S(1)} %get-tuple-element.7), channel_id=1, replica_groups=mesh['freq'=8,'sx'=16,'sy'=4] {'freq'}, dimensions={0}, use_global_device_ids=true | all-gather | bytes 442368 | tf_op jit(solution)/shard_map/all_gather | solution.py:69
  839.2 11.0 all_to_all.35
  851.8 4.8 collective-permute-start.22
  865.3 126.1 %psum.61 = f32[4]{0:T(128)S(1)} all-reduce(f32[4]{0:T(128)S(1)} %multiply_reduce_fusion.1), channel_id=1, replica_groups=mesh['freq'=8,'sx'=16,'sy'=4] {'sx','sy'}, use_global_device_ids=true, to_apply=%region_12.13 | all-reduce | flops 4 | bytes 32 | tf_op jit(solution)/shard_map/psum | solution.py:93
  992.0 25.7 %all_gather.34 = bf16[32,2,4,768]{3,2,1,0:T(4,128)(2,1)S(1)} all-gather(bf16[4,2,4,768]{3,2,1,0:T(4,128)(2,1)S(1)} %subtract_convert_fusion), channel_id=1, replica_groups=mesh['freq'=8,'sx'=16,'sy'=4] {'freq'}, dimensions={0}, use_global_device_ids=true | all-gather | bytes 442368 | tf_op jit(solution)/shard_map/all_gather | solution.py:69
  1020.7 10.8 all_to_all.36
  1046.3 124.3 %psum.62 = f32[4]{0:T(128)S(1)} all-reduce(f32[4]{0:T(128)S(1)} %multiply_reduce_fusion), channel_id=1, replica_groups=mesh['freq'=8,'sx'=16,'sy'=4] {'sx','sy'}, use_global_device_ids=true, to_apply=%region_14.15 | all-reduce | flops 4 | bytes 32 | tf_op jit(solution)/shard_map/psum | solution.py:93
  1171.2 25.0 %all_gather.35 = bf16[32,2,4,768]{3,2,1,0:T(4,128)(2,1)S(1)} all-gather(bf16[4,2,4,768]{3,2,1,0:T(4,128)(2,1)S(1)} %fusion.68), channel_id=1, replica_groups=mesh['freq'=8,'sx'=16,'sy'=4] {'freq'}, dimensions={0}, use_global_device_ids=true | all-gather | bytes 442368 | tf_op jit(solution)/shard_map/all_gather | solution.py:69
  1203.5 8.2 all-to-all-done.7
  1213.2 4.7 collective-permute-start.30
  1227.3 126.1 %psum.63 = f32[4]{0:T(128)S(1)} all-reduce(f32[4]{0:T(128)S(1)} %fusion.65), channel_id=1, replica_groups=mesh['freq'=8,'sx'=16,'sy'=4] {'sx','sy'}, use_global_device_ids=true, to_apply=%region_16.17 | all-reduce | flops 4 | bytes 32 | tf_op jit(solution)/shard_map/psum | solution.py:93
  1354.2 16.8 %scatter_custom_fusion = f32[1728]{0:T(1024)S(1)} fusion(s32[3072]{0:T(1024)S(1)} %reshape.442, f32[3072]{0:T(1024)S(1)} %reshape.444, f32[]{:T(128)} %constant.14.clone.1), kind=kCustom, calls=%fused_computation.212 | custom fusion | flops 3072 | bytes 6916 | tf_op jit(solution)/shard_map/scatter-add | solution.py:152
  1371.0 15.0 %all-reduce.1 = f32[1728]{0:T(1024)S(1)} all-reduce(f32[1728]{0:T(1024)S(1)} %broadcast_multiply_fusion), channel_id=2, replica_groups=mesh['freq'=8,'sx'=16,'sy'=4] {'freq'}, use_global_device_ids=true, to_apply=%region_19.20.clone | all-reduce | flops 1728 | bytes 13824
  (303 shorter events, 142.2 us)
Async XLA Ops:
  66.1 11.7 all-to-all-start
  78.0 10.2 collective-permute-start.1
  80.0 8.3 collective-permute-start
  82.4 5.9 collective-permute-start.3
  83.7 6.1 collective-permute-start.2
  118.9 11.7 all-to-all-start.1
  130.8 10.7 collective-permute-start.7
  132.1 9.4 collective-permute-start.6
  139.0 6.4 collective-permute-start.4
  311.6 10.2 collective-permute-start.11
  312.9 9.0 collective-permute-start.10
  317.5 4.5 collective-permute-start.9
  319.4 6.4 collective-permute-start.8
  490.3 10.8 collective-permute-start.15
  491.6 9.5 collective-permute-start.14
  496.7 4.5 collective-permute-start.13
  498.6 6.4 collective-permute-start.12
  671.7 10.2 collective-permute-start.19
  673.0 9.0 collective-permute-start.18
  677.6 4.5 collective-permute-start.17
  679.6 6.4 collective-permute-start.16
  850.5 10.5 collective-permute-start.23
  851.8 9.2 collective-permute-start.22
  856.6 4.5 collective-permute-start.21
  858.6 6.4 collective-permute-start.20
  1031.7 10.2 collective-permute-start.27
  1033.0 9.0 collective-permute-start.26
  1039.6 6.4 collective-permute-start.24
  1200.0 11.7 all-to-all-start.7
  1211.9 10.4 collective-permute-start.31
  1213.2 9.1 collective-permute-start.30
  1219.9 6.4 collective-permute-start.28
  (49 other events, 3992.7 us)
where the time goes:
time: 1390 us
  blocking collectives  1170 us (84%)
  starting transfers between devices  92.8 us (7%)
  waiting for transfers between devices  52.5 us (4%)
  other arithmetic  25.2 us (2%)
  local copies, waits for them, and re-layouts  23 us (2%)
  matrix products  18.9 us (1%)
    psum x7, blocking collectives, reduce_dots(): summed = lax.psum(partial_value, ('sx', 'sy'))  877 us
    all_gather x8, blocking collectives, apply_rows(): pieces = lax.all_gather(rounded, 'freq', axis=0, tiled=True)  208 us
    ppermute x16, starting transfers between devices, padded(): lax.ppermute(tail, axis, [(i, (i + 1) % count) for i in range(ends)])  57 us
    all_to_all x5, blocking collectives, apply_rows(): lax.all_to_all(local_vals.astype(jnp.bfloat16), 'freq', split_axis=0, con...  54.3 us
    unnamed x2, blocking collectives  32 us
  transfers between devices with their start and end apart: 35, of which 11 were waited for; matrix products, arithmetic and copies ran while one was open for 0% of the time, Pallas kernels for 0%

commit v1 on v0

--- a/solution.py
+++ b/solution.py
@@ -90,7 +90,7 @@
             for first_vec, second_vec in factor_pairs
         )
     )
-    summed = lax.psum(partial_value, ("sx", "sy"))
+    summed = lax.psum(lax.psum(partial_value, "sy"), "sx")
     return summed
 
 

time: 1390 us -> 738 us (0.53)
  blocking collectives: 1170 us -> 521 us
    psum x7 -> x14, blocking collectives: 877 us -> 227 us  [reduce_dots(): summed = lax.psum(lax.psum(partial_value, 'sy'), 'sx')]
where the time goes in v1:
time: 738 us; the launch traced here: 736 us
  blocking collectives  521 us (71%)
  starting transfers between devices  91.8 us (12%)
  waiting for transfers between devices  52.5 us (7%)
  other arithmetic  25.2 us (3%)
  local copies, waits for them, and re-layouts  23 us (3%)
  matrix products  18.9 us (3%)
    psum x14, blocking collectives, reduce_dots(): summed = lax.psum(lax.psum(partial_value, 'sy'), 'sx')  227 us
    all_gather x8, blocking collectives, apply_rows(): pieces = lax.all_gather(rounded, 'freq', axis=0, tiled=True)  208 us
    ppermute x16, starting transfers between devices, padded(): lax.ppermute(tail, axis, [(i, (i + 1) % count) for i in range(ends)])  56.1 us
    all_to_all x5, blocking collectives, apply_rows(): lax.all_to_all(local_vals.astype(jnp.bfloat16), 'freq', split_axis=0, con...  54.6 us
    unnamed x2, blocking collectives  32 us
    ppermute x16, waiting for transfers between devices, padded(): lax.ppermute(tail, axis, [(i, (i + 1) % count) for i in range(ends)])  27.7 us
    ppermute x16, starting transfers between devices, padded(): lax.ppermute(head, axis, [((i + 1) % count, i) for i in range(ends)])  25.7 us
    all_to_all x3, waiting for transfers between devices, apply_rows(): lax.all_to_all(local_vals.astype(jnp.bfloat16), 'freq', split_axis=0, con...  24.8 us
  transfers between devices with their start and end apart: 35, of which 11 were waited for; matrix products, arithmetic and copies ran while one was open for 0% of the time, Pallas kernels for 0%

profile of v1, /device:TPU:32, one launch (start us, length us, event | category | flops | bytes accessed | tf_op | source)
XLA Modules:
  0.0 736.2 jit_solution(10709400802163857110)
XLA Ops:
  5.8 31.4 %all_gather.27 = bf16[32,2,4,768]{3,2,1,0:T(4,128)(2,1)S(1)} all-gather(bf16[4,2,4,768]{3,2,1,0:T(4,128)(2,1)S(1)} %bitcast_convert_fusion), channel_id=1, replica_groups=mesh['freq'=8,'sx'=16,'sy'=4] {'freq'}, dimensions={0}, use_global_device_ids=true | all-gather | bytes 442368 | tf_op jit(solution)/shard_map/all_gather | solution.py:69
  48.3 17.0 %all-reduce = f32[32]{0:T(128)S(1)} all-reduce(f32[32]{0:T(128)S(1)} %dynamic-update-slice), channel_id=1, replica_groups=mesh['freq'=8,'sx'=16,'sy'=4] {'freq'}, use_global_device_ids=true, to_apply=%add | all-reduce | flops 32 | bytes 256
  69.5 8.3 %all-to-all-done = bf16[32,2,4,96]{3,2,1,0:T(4,128)(2,1)S(1)} async-done(((bf16[32,2,4,96]{3,2,1,0:T(4,128)(2,1)}), bf16[32,2,4,96]{3,2,1,0:T(4,128)(2,1)S(1)}, u32[]{:S(2)}, u32[]{:S(2)}) %all-to-all-start) | async-done | bytes 49184 | tf_op jit(solution)/shard_map/all_to_all | solution.py:80
  90.1 25.1 %all_gather.29 = bf16[32,2,4,768]{3,2,1,0:T(4,128)(2,1)S(1)} all-gather(bf16[4,2,4,768]{3,2,1,0:T(4,128)(2,1)S(1)} %fusion.103), channel_id=1, replica_groups=mesh['freq'=8,'sx'=16,'sy'=4] {'freq'}, dimensions={0}, use_global_device_ids=true | all-gather | bytes 442368 | tf_op jit(solution)/shard_map/all_gather | solution.py:69
  145.8 9.7 %all-reduce.3 = (f32[4]{0:T(128)S(1)}, f32[4]{0:T(128)S(1)}) all-reduce(f32[4]{0:T(128)S(1)} %get-tuple-element.4, f32[4]{0:T(128)S(1)} %get-tuple-element.3), channel_id=1, replica_groups=mesh['freq'=8,'sx'=16,'sy'=4] {'sy'}, use_global_device_ids=true, to_apply=%region_2.3 | all-reduce | flops 8 | bytes 64 | tf_op jit(solution)/shard_map/psum | solution.py:93
  155.6 23.5 %all-reduce.2 = (f32[4]{0:T(128)S(1)}, f32[4]{0:T(128)S(1)}) all-reduce(f32[4]{0:T(128)S(1)} %get-tuple-element.7, f32[4]{0:T(128)S(1)} %get-tuple-element.8), channel_id=1, replica_groups=mesh['freq'=8,'sx'=16,'sy'=4] {'sx'}, use_global_device_ids=true, to_apply=%region_3.4 | all-reduce | flops 8 | bytes 64 | tf_op jit(solution)/shard_map/psum | solution.py:93
  179.2 25.2 %all_gather.30 = bf16[32,2,4,768]{3,2,1,0:T(4,128)(2,1)S(1)} all-gather(bf16[4,2,4,768]{3,2,1,0:T(4,128)(2,1)S(1)} %get-tuple-element.15), channel_id=1, replica_groups=mesh['freq'=8,'sx'=16,'sy'=4] {'freq'}, dimensions={0}, use_global_device_ids=true | all-gather | bytes 442368 | tf_op jit(solution)/shard_map/all_gather | solution.py:69
  207.5 10.9 %all_to_all.32 = bf16[32,2,4,96]{3,2,1,0:T(4,128)(2,1)S(1)} all-to-all(bf16[32,2,4,96]{3,2,1,0:T(4,128)(2,1)S(1)} %copy.85), channel_id=1, replica_groups=mesh['freq'=8,'sx'=16,'sy'=4] {'freq'}, dimensions={0} | all-to-all | bytes 98304 | tf_op jit(solution)/shard_map/all_to_all | solution.py:80
  233.2 8.8 %psum.116 = f32[4]{0:T(128)S(1)} all-reduce(f32[4]{0:T(128)S(1)} %multiply_reduce_fusion.4), channel_id=1, replica_groups=mesh['freq'=8,'sx'=16,'sy'=4] {'sy'}, use_global_device_ids=true, to_apply=%region_8.9 | all-reduce | flops 4 | bytes 32 | tf_op jit(solution)/shard_map/psum | solution.py:93
  241.9 23.5 %psum.117 = f32[4]{0:T(128)S(1)} all-reduce(f32[4]{0:T(128)S(1)} %psum.116), channel_id=1, replica_groups=mesh['freq'=8,'sx'=16,'sy'=4] {'sx'}, use_global_device_ids=true, to_apply=%region_9.10 | all-reduce | flops 4 | bytes 32 | tf_op jit(solution)/shard_map/psum | solution.py:93
  265.7 25.2 %all_gather.31 = bf16[32,2,4,768]{3,2,1,0:T(4,128)(2,1)S(1)} all-gather(bf16[4,2,4,768]{3,2,1,0:T(4,128)(2,1)S(1)} %get-tuple-element.13), channel_id=1, replica_groups=mesh['freq'=8,'sx'=16,'sy'=4] {'freq'}, dimensions={0}, use_global_device_ids=true | all-gather | bytes 442368 | tf_op jit(solution)/shard_map/all_gather | solution.py:69
  294.0 10.9 %all_to_all.33 = bf16[32,2,4,96]{3,2,1,0:T(4,128)(2,1)S(1)} all-to-all(bf16[32,2,4,96]{3,2,1,0:T(4,128)(2,1)S(1)} %copy.88), channel_id=1, replica_groups=mesh['freq'=8,'sx'=16,'sy'=4] {'freq'}, dimensions={0} | all-to-all | bytes 98304 | tf_op jit(solution)/shard_map/all_to_all | solution.py:80
  319.7 8.9 %psum.118 = f32[4]{0:T(128)S(1)} all-reduce(f32[4]{0:T(128)S(1)} %multiply_reduce_fusion.3), channel_id=1, replica_groups=mesh['freq'=8,'sx'=16,'sy'=4] {'sy'}, use_global_device_ids=true, to_apply=%region_11.12 | all-reduce | flops 4 | bytes 32 | tf_op jit(solution)/shard_map/psum | solution.py:93
  328.5 23.5 %psum.119 = f32[4]{0:T(128)S(1)} all-reduce(f32[4]{0:T(128)S(1)} %psum.118), channel_id=1, replica_groups=mesh['freq'=8,'sx'=16,'sy'=4] {'sx'}, use_global_device_ids=true, to_apply=%region_12.13 | all-reduce | flops 4 | bytes 32 | tf_op jit(solution)/shard_map/psum | solution.py:93
  352.8 25.2 %all_gather.32 = bf16[32,2,4,768]{3,2,1,0:T(4,128)(2,1)S(1)} all-gather(bf16[4,2,4,768]{3,2,1,0:T(4,128)(2,1)S(1)} %get-tuple-element.11), channel_id=1, replica_groups=mesh['freq'=8,'sx'=16,'sy'=4] {'freq'}, dimensions={0}, use_global_device_ids=true | all-gather | bytes 442368 | tf_op jit(solution)/shard_map/all_gather | solution.py:69
  381.1 10.9 %all_to_all.34 = bf16[32,2,4,96]{3,2,1,0:T(4,128)(2,1)S(1)} all-to-all(bf16[32,2,4,96]{3,2,1,0:T(4,128)(2,1)S(1)} %copy.91), channel_id=1, replica_groups=mesh['freq'=8,'sx'=16,'sy'=4] {'freq'}, dimensions={0} | all-to-all | bytes 98304 | tf_op jit(solution)/shard_map/all_to_all | solution.py:80
  406.8 8.6 %psum.120 = f32[4]{0:T(128)S(1)} all-reduce(f32[4]{0:T(128)S(1)} %multiply_reduce_fusion.2), channel_id=1, replica_groups=mesh['freq'=8,'sx'=16,'sy'=4] {'sy'}, use_global_device_ids=true, to_apply=%region_14.15 | all-reduce | flops 4 | bytes 32 | tf_op jit(solution)/shard_map/psum | solution.py:93
  415.4 23.5 %psum.121 = f32[4]{0:T(128)S(1)} all-reduce(f32[4]{0:T(128)S(1)} %psum.120), channel_id=1, replica_groups=mesh['freq'=8,'sx'=16,'sy'=4] {'sx'}, use_global_device_ids=true, to_apply=%region_15.16 | all-reduce | flops 4 | bytes 32 | tf_op jit(solution)/shard_map/psum | solution.py:93
  439.5 25.1 %all_gather.33 = bf16[32,2,4,768]{3,2,1,0:T(4,128)(2,1)S(1)} all-gather(bf16[4,2,4,768]{3,2,1,0:T(4,128)(2,1)S(1)} %get-tuple-element.9), channel_id=1, replica_groups=mesh['freq'=8,'sx'=16,'sy'=4] {'freq'}, dimensions={0}, use_global_device_ids=true | all-gather | bytes 442368 | tf_op jit(solution)/shard_map/all_gather | solution.py:69
  467.7 10.9 %all_to_all.35 = bf16[32,2,4,96]{3,2,1,0:T(4,128)(2,1)S(1)} all-to-all(bf16[32,2,4,96]{3,2,1,0:T(4,128)(2,1)S(1)} %copy.94), channel_id=1, replica_groups=mesh['freq'=8,'sx'=16,'sy'=4] {'freq'}, dimensions={0} | all-to-all | bytes 98304 | tf_op jit(solution)/shard_map/all_to_all | solution.py:80
  493.4 8.9 %psum.122 = f32[4]{0:T(128)S(1)} all-reduce(f32[4]{0:T(128)S(1)} %multiply_reduce_fusion.1), channel_id=1, replica_groups=mesh['freq'=8,'sx'=16,'sy'=4] {'sy'}, use_global_device_ids=true, to_apply=%region_17.18 | all-reduce | flops 4 | bytes 32 | tf_op jit(solution)/shard_map/psum | solution.py:93
  502.2 23.5 %psum.123 = f32[4]{0:T(128)S(1)} all-reduce(f32[4]{0:T(128)S(1)} %psum.122), channel_id=1, replica_groups=mesh['freq'=8,'sx'=16,'sy'=4] {'sx'}, use_global_device_ids=true, to_apply=%region_18.19 | all-reduce | flops 4 | bytes 32 | tf_op jit(solution)/shard_map/psum | solution.py:93
  526.4 25.4 %all_gather.34 = bf16[32,2,4,768]{3,2,1,0:T(4,128)(2,1)S(1)} all-gather(bf16[4,2,4,768]{3,2,1,0:T(4,128)(2,1)S(1)} %subtract_convert_fusion), channel_id=1, replica_groups=mesh['freq'=8,'sx'=16,'sy'=4] {'freq'}, dimensions={0}, use_global_device_ids=true | all-gather | bytes 442368 | tf_op jit(solution)/shard_map/all_gather | solution.py:69
  554.8 10.9 %all_to_all.36 = bf16[32,2,4,96]{3,2,1,0:T(4,128)(2,1)S(1)} all-to-all(bf16[32,2,4,96]{3,2,1,0:T(4,128)(2,1)S(1)} %copy.97), channel_id=1, replica_groups=mesh['freq'=8,'sx'=16,'sy'=4] {'freq'}, dimensions={0} | all-to-all | bytes 98304 | tf_op jit(solution)/shard_map/all_to_all | solution.py:80
  580.5 8.6 %psum.124 = f32[4]{0:T(128)S(1)} all-reduce(f32[4]{0:T(128)S(1)} %multiply_reduce_fusion), channel_id=1, replica_groups=mesh['freq'=8,'sx'=16,'sy'=4] {'sy'}, use_global_device_ids=true, to_apply=%region_20.21 | all-reduce | flops 4 | bytes 32 | tf_op jit(solution)/shard_map/psum | solution.py:93
  589.1 23.5 %psum.125 = f32[4]{0:T(128)S(1)} all-reduce(f32[4]{0:T(128)S(1)} %psum.124), channel_id=1, replica_groups=mesh['freq'=8,'sx'=16,'sy'=4] {'sx'}, use_global_device_ids=true, to_apply=%region_21.22 | all-reduce | flops 4 | bytes 32 | tf_op jit(solution)/shard_map/psum | solution.py:93
  613.3 25.2 %all_gather.35 = bf16[32,2,4,768]{3,2,1,0:T(4,128)(2,1)S(1)} all-gather(bf16[4,2,4,768]{3,2,1,0:T(4,128)(2,1)S(1)} %fusion.68), channel_id=1, replica_groups=mesh['freq'=8,'sx'=16,'sy'=4] {'freq'}, dimensions={0}, use_global_device_ids=true | all-gather | bytes 442368 | tf_op jit(solution)/shard_map/all_gather | solution.py:69
  645.7 8.3 %all-to-all-done.7 = bf16[32,2,4,96]{3,2,1,0:T(4,128)(2,1)S(1)} async-done(((bf16[32,2,4,96]{3,2,1,0:T(4,128)(2,1)}), bf16[32,2,4,96]{3,2,1,0:T(4,128)(2,1)S(1)}, u32[]{:S(2)}, u32[]{:S(2)}) %all-to-all-start.7) | async-done | bytes 49184 | tf_op jit(solution)/shard_map/all_to_all | solution.py:80
  668.7 8.9 %psum.126 = f32[4]{0:T(128)S(1)} all-reduce(f32[4]{0:T(128)S(1)} %fusion.65), channel_id=1, replica_groups=mesh['freq'=8,'sx'=16,'sy'=4] {'sy'}, use_global_device_ids=true, to_apply=%region_23.24 | all-reduce | flops 4 | bytes 32 | tf_op jit(solution)/shard_map/psum | solution.py:93
  678.3 23.6 %psum.127 = f32[4]{0:T(128)S(1)} all-reduce(f32[4]{0:T(128)S(1)} %psum.126), channel_id=1, replica_groups=mesh['freq'=8,'sx'=16,'sy'=4] {'sx'}, use_global_device_ids=true, to_apply=%region_24.25 | all-reduce | flops 4 | bytes 32 | tf_op jit(solution)/shard_map/psum | solution.py:93
  702.6 16.8 %scatter_custom_fusion = f32[1728]{0:T(1024)S(1)} fusion(s32[3072]{0:T(1024)S(1)} %reshape.442, f32[3072]{0:T(1024)S(1)} %reshape.444, f32[]{:T(128)} %constant.14.clone.1), kind=kCustom, calls=%fused_computation.212 | custom fusion | flops 3072 | bytes 6916 | tf_op jit(solution)/shard_map/scatter-add | solution.py:152
  719.4 15.0 %all-reduce.1 = f32[1728]{0:T(1024)S(1)} all-reduce(f32[1728]{0:T(1024)S(1)} %broadcast_multiply_fusion), channel_id=2, replica_groups=mesh['freq'=8,'sx'=16,'sy'=4] {'freq'}, use_global_device_ids=true, to_apply=%region_27.28.clone | all-reduce | flops 1728 | bytes 13824
  (310 shorter events, 178.0 us)
Async XLA Ops:
  66.1 11.7 %all-to-all-start = ((bf16[32,2,4,96]{3,2,1,0:T(4,128)(2,1)}), bf16[32,2,4,96]{3,2,1,0:T(4,128)(2,1)S(1)}, u32[]{:S(2)}, u32[]{:S(2)}) async-start(bf16[32,2,4,96]{3,2,1,0:T(4,128)(2,1)} %copy.79), calls=%async_computation | async-start | bytes 131072 | tf_op jit(solution)/shard_map/all_to_all | solution.py:80
  78.0 10.2 %collective-permute-start.1 = (bf16[4,2,1,768]{3,2,1,0:T(2,128)(2,1)S(1)}, bf16[4,2,1,768]{3,2,1,0:T(2,128)(2,1)S(1)}, u32[]{:S(2)}, u32[]{:S(2)}) collective-permute-start(bf16[4,2,1,768]{3,2,1,0:T(2,128)(2,1)S(1)} %get-tuple-element.110), channel_id=1, source_target_pairs={{4,0},{8,4},{12,8},{16,12},{20,16},{24,20},{28,24},{32,28},{36,32}... | collective-permute-start | bytes 36872 | tf_op jit(solution)/shard_map/ppermute | solution.py:21
  79.9 8.3 %collective-permute-start = (bf16[4,2,1,768]{3,2,1,0:T(2,128)(2,1)S(1)}, bf16[4,2,1,768]{3,2,1,0:T(2,128)(2,1)S(1)}, u32[]{:S(2)}, u32[]{:S(2)}) collective-permute-start(bf16[4,2,1,768]{3,2,1,0:T(2,128)(2,1)S(1)} %get-tuple-element.107), channel_id=1, source_target_pairs={{0,4},{4,8},{8,12},{12,16},{16,20},{20,24},{24,28},{28,32},{32,36}... | collective-permute-start | bytes 36872 | tf_op jit(solution)/shard_map/ppermute | solution.py:19
  82.3 5.9 collective-permute-start.3
  83.6 6.1 collective-permute-start.2
  118.8 11.7 %all-to-all-start.1 = ((bf16[32,2,4,96]{3,2,1,0:T(4,128)(2,1)}), bf16[32,2,4,96]{3,2,1,0:T(4,128)(2,1)S(1)}, u32[]{:S(2)}, u32[]{:S(2)}) async-start(bf16[32,2,4,96]{3,2,1,0:T(4,128)(2,1)} %copy.82), calls=%async_computation.1 | async-start | bytes 131072 | tf_op jit(solution)/shard_map/all_to_all | solution.py:80
  130.7 10.7 %collective-permute-start.7 = (bf16[4,2,1,768]{3,2,1,0:T(2,128)(2,1)S(1)}, bf16[4,2,1,768]{3,2,1,0:T(2,128)(2,1)S(1)}, u32[]{:S(2)}, u32[]{:S(2)}) collective-permute-start(bf16[4,2,1,768]{3,2,1,0:T(2,128)(2,1)S(1)} %get-tuple-element.102), channel_id=1, source_target_pairs={{1,0},{2,1},{3,2},{5,4},{6,5},{7,6},{9,8},{10,9},{11,10},{13,12},{... | collective-permute-start | bytes 36872 | tf_op jit(solution)/shard_map/ppermute | solution.py:21
  132.0 9.4 %collective-permute-start.6 = (bf16[4,2,1,768]{3,2,1,0:T(2,128)(2,1)S(1)}, bf16[4,2,1,768]{3,2,1,0:T(2,128)(2,1)S(1)}, u32[]{:S(2)}, u32[]{:S(2)}) collective-permute-start(bf16[4,2,1,768]{3,2,1,0:T(2,128)(2,1)S(1)} %get-tuple-element.103), channel_id=1, source_target_pairs={{0,1},{1,2},{2,3},{4,5},{5,6},{6,7},{8,9},{9,10},{10,11},{12,13},{... | collective-permute-start | bytes 36872 | tf_op jit(solution)/shard_map/ppermute | solution.py:19
  137.1 4.5 collective-permute-start.5
  139.0 6.4 collective-permute-start.4
  218.6 10.2 %collective-permute-start.11 = (bf16[4,2,1,768]{3,2,1,0:T(2,128)(2,1)S(1)}, bf16[4,2,1,768]{3,2,1,0:T(2,128)(2,1)S(1)}, u32[]{:S(2)}, u32[]{:S(2)}) collective-permute-start(bf16[4,2,1,768]{3,2,1,0:T(2,128)(2,1)S(1)} %get-tuple-element.96), channel_id=1, source_target_pairs={{1,0},{2,1},{3,2},{5,4},{6,5},{7,6},{9,8},{10,9},{11,10},{13,12},{... | collective-permute-start | bytes 36872 | tf_op jit(solution)/shard_map/ppermute | solution.py:21
  219.9 9.0 %collective-permute-start.10 = (bf16[4,2,1,768]{3,2,1,0:T(2,128)(2,1)S(1)}, bf16[4,2,1,768]{3,2,1,0:T(2,128)(2,1)S(1)}, u32[]{:S(2)}, u32[]{:S(2)}) collective-permute-start(bf16[4,2,1,768]{3,2,1,0:T(2,128)(2,1)S(1)} %get-tuple-element.97), channel_id=1, source_target_pairs={{0,1},{1,2},{2,3},{4,5},{5,6},{6,7},{8,9},{9,10},{10,11},{12,13},{... | collective-permute-start | bytes 36872 | tf_op jit(solution)/shard_map/ppermute | solution.py:19
  224.5 4.5 collective-permute-start.9
  226.4 6.4 collective-permute-start.8
  305.1 10.2 %collective-permute-start.15 = (bf16[4,2,1,768]{3,2,1,0:T(2,128)(2,1)S(1)}, bf16[4,2,1,768]{3,2,1,0:T(2,128)(2,1)S(1)}, u32[]{:S(2)}, u32[]{:S(2)}) collective-permute-start(bf16[4,2,1,768]{3,2,1,0:T(2,128)(2,1)S(1)} %get-tuple-element.90), channel_id=1, source_target_pairs={{1,0},{2,1},{3,2},{5,4},{6,5},{7,6},{9,8},{10,9},{11,10},{13,12},{... | collective-permute-start | bytes 36872 | tf_op jit(solution)/shard_map/ppermute | solution.py:21
  306.4 9.0 %collective-permute-start.14 = (bf16[4,2,1,768]{3,2,1,0:T(2,128)(2,1)S(1)}, bf16[4,2,1,768]{3,2,1,0:T(2,128)(2,1)S(1)}, u32[]{:S(2)}, u32[]{:S(2)}) collective-permute-start(bf16[4,2,1,768]{3,2,1,0:T(2,128)(2,1)S(1)} %get-tuple-element.91), channel_id=1, source_target_pairs={{0,1},{1,2},{2,3},{4,5},{5,6},{6,7},{8,9},{9,10},{10,11},{12,13},{... | collective-permute-start | bytes 36872 | tf_op jit(solution)/shard_map/ppermute | solution.py:19
  311.0 4.5 collective-permute-start.13
  312.9 6.4 collective-permute-start.12
  392.2 10.2 %collective-permute-start.19 = (bf16[4,2,1,768]{3,2,1,0:T(2,128)(2,1)S(1)}, bf16[4,2,1,768]{3,2,1,0:T(2,128)(2,1)S(1)}, u32[]{:S(2)}, u32[]{:S(2)}) collective-permute-start(bf16[4,2,1,768]{3,2,1,0:T(2,128)(2,1)S(1)} %get-tuple-element.84), channel_id=1, source_target_pairs={{1,0},{2,1},{3,2},{5,4},{6,5},{7,6},{9,8},{10,9},{11,10},{13,12},{... | collective-permute-start | bytes 36872 | tf_op jit(solution)/shard_map/ppermute | solution.py:21
  393.5 9.0 %collective-permute-start.18 = (bf16[4,2,1,768]{3,2,1,0:T(2,128)(2,1)S(1)}, bf16[4,2,1,768]{3,2,1,0:T(2,128)(2,1)S(1)}, u32[]{:S(2)}, u32[]{:S(2)}) collective-permute-start(bf16[4,2,1,768]{3,2,1,0:T(2,128)(2,1)S(1)} %get-tuple-element.85), channel_id=1, source_target_pairs={{0,1},{1,2},{2,3},{4,5},{5,6},{6,7},{8,9},{9,10},{10,11},{12,13},{... | collective-permute-start | bytes 36872 | tf_op jit(solution)/shard_map/ppermute | solution.py:19
  398.1 4.5 collective-permute-start.17
  400.0 6.4 collective-permute-start.16
  478.8 10.2 %collective-permute-start.23 = (bf16[4,2,1,768]{3,2,1,0:T(2,128)(2,1)S(1)}, bf16[4,2,1,768]{3,2,1,0:T(2,128)(2,1)S(1)}, u32[]{:S(2)}, u32[]{:S(2)}) collective-permute-start(bf16[4,2,1,768]{3,2,1,0:T(2,128)(2,1)S(1)} %get-tuple-element.78), channel_id=1, source_target_pairs={{1,0},{2,1},{3,2},{5,4},{6,5},{7,6},{9,8},{10,9},{11,10},{13,12},{... | collective-permute-start | bytes 36872 | tf_op jit(solution)/shard_map/ppermute | solution.py:21
  480.1 9.0 %collective-permute-start.22 = (bf16[4,2,1,768]{3,2,1,0:T(2,128)(2,1)S(1)}, bf16[4,2,1,768]{3,2,1,0:T(2,128)(2,1)S(1)}, u32[]{:S(2)}, u32[]{:S(2)}) collective-permute-start(bf16[4,2,1,768]{3,2,1,0:T(2,128)(2,1)S(1)} %get-tuple-element.79), channel_id=1, source_target_pairs={{0,1},{1,2},{2,3},{4,5},{5,6},{6,7},{8,9},{9,10},{10,11},{12,13},{... | collective-permute-start | bytes 36872 | tf_op jit(solution)/shard_map/ppermute | solution.py:19
  486.6 6.4 collective-permute-start.20
  566.0 10.2 %collective-permute-start.27 = (bf16[4,2,1,768]{3,2,1,0:T(2,128)(2,1)S(1)}, bf16[4,2,1,768]{3,2,1,0:T(2,128)(2,1)S(1)}, u32[]{:S(2)}, u32[]{:S(2)}) collective-permute-start(bf16[4,2,1,768]{3,2,1,0:T(2,128)(2,1)S(1)} %get-tuple-element.72), channel_id=1, source_target_pairs={{1,0},{2,1},{3,2},{5,4},{6,5},{7,6},{9,8},{10,9},{11,10},{13,12},{... | collective-permute-start | bytes 36872 | tf_op jit(solution)/shard_map/ppermute | solution.py:21
  567.3 9.0 %collective-permute-start.26 = (bf16[4,2,1,768]{3,2,1,0:T(2,128)(2,1)S(1)}, bf16[4,2,1,768]{3,2,1,0:T(2,128)(2,1)S(1)}, u32[]{:S(2)}, u32[]{:S(2)}) collective-permute-start(bf16[4,2,1,768]{3,2,1,0:T(2,128)(2,1)S(1)} %get-tuple-element.73), channel_id=1, source_target_pairs={{0,1},{1,2},{2,3},{4,5},{5,6},{6,7},{8,9},{9,10},{10,11},{12,13},{... | collective-permute-start | bytes 36872 | tf_op jit(solution)/shard_map/ppermute | solution.py:19
  573.8 6.4 collective-permute-start.24
  642.3 11.7 %all-to-all-start.7 = ((bf16[32,2,4,96]{3,2,1,0:T(4,128)(2,1)}), bf16[32,2,4,96]{3,2,1,0:T(4,128)(2,1)S(1)}, u32[]{:S(2)}, u32[]{:S(2)}) async-start(bf16[32,2,4,96]{3,2,1,0:T(4,128)(2,1)} %copy.100), calls=%async_computation.7 | async-start | bytes 131072 | tf_op jit(solution)/shard_map/all_to_all | solution.py:80
  654.2 10.2 %collective-permute-start.31 = (bf16[4,2,1,768]{3,2,1,0:T(2,128)(2,1)S(1)}, bf16[4,2,1,768]{3,2,1,0:T(2,128)(2,1)S(1)}, u32[]{:S(2)}, u32[]{:S(2)}) collective-permute-start(bf16[4,2,1,768]{3,2,1,0:T(2,128)(2,1)S(1)} %get-tuple-element.66), channel_id=1, source_target_pairs={{1,0},{2,1},{3,2},{5,4},{6,5},{7,6},{9,8},{10,9},{11,10},{13,12},{... | collective-permute-start | bytes 36872 | tf_op jit(solution)/shard_map/ppermute | solution.py:21
  655.5 9.0 %collective-permute-start.30 = (bf16[4,2,1,768]{3,2,1,0:T(2,128)(2,1)S(1)}, bf16[4,2,1,768]{3,2,1,0:T(2,128)(2,1)S(1)}, u32[]{:S(2)}, u32[]{:S(2)}) collective-permute-start(bf16[4,2,1,768]{3,2,1,0:T(2,128)(2,1)S(1)} %get-tuple-element.67), channel_id=1, source_target_pairs={{0,1},{1,2},{2,3},{4,5},{5,6},{6,7},{8,9},{9,10},{10,11},{12,13},{... | collective-permute-start | bytes 36872 | tf_op jit(solution)/shard_map/ppermute | solution.py:19
  662.0 6.4 collective-permute-start.28
  (49 other events, 1781.6 us)
